TPU v7x, 32 devices: a whole 2x2x4 slice. The times are simulated.
32 devices in a mesh: team: 4 (over z), blk: 4 (over y, x), head: 2 (over core).
Axes of the slice: x: 2, y: 2, z: 4, core: 2. Of those that a mesh axis runs over, the one named last changes fastest.
Arguments:
- query: bfloat16 [2048, 2560], P(('team', 'blk'), 'head'), parts along dimension 1, may hold values from -15 to 15
- keys: bfloat16 [2048, 2560], P(('team', 'blk'), 'head'), parts along dimension 1, may hold values from -6 to 6
- values: bfloat16 [2048, 2560], P(('team', 'blk'), 'head'), parts along dimension 1, may hold values from -6 to 6
Outputs:
- attended: bfloat16 [2048, 2560], P(('team', 'blk'), 'head'), parts along dimension 1
There are 2 independent parts, one for each index of `head`. A program takes and returns all parts, laid end to end along the dimension named above; each array names one. Nothing has to cross between parts.
All inputs are finite; a program needn't handle non-finite values.
Results may differ from a plain program's by a relative error of at most 0.006.
Values may be sent and summed in bfloat16 or wider, within the bound.
A program may use at most 128 MiB of HBM per device.

v0:
```python
import math
import jax
import jax.numpy as jnp
from jax import lax
from jax.sharding import PartitionSpec as P

HEAD_DIM = 128


def shifted(value, axis, by):
    count = lax.axis_size(axis)
    return lax.ppermute(value, axis, [(i, (i + by) % count) for i in range(count)])


def on_device(query, keys, values):
    shard_rows = query.shape[0]
    feature_width = query.shape[1]
    head_count = feature_width // HEAD_DIM
    score_scale = 1.0 / math.sqrt(HEAD_DIM)
    team_query = lax.all_gather(query, "team", axis=0, tiled=True)
    team_heads = team_query.reshape(-1, head_count, HEAD_DIM)

    def scores_of(key_block):
        key_heads = key_block.reshape(shard_rows, head_count, HEAD_DIM)
        return (
            jnp.einsum("qhd,khd->qhk", team_heads, key_heads, preferred_element_type=jnp.float32)
            * score_scale
        )

    def weighted(weights, value_block):
        value_heads = value_block.reshape(shard_rows, head_count, HEAD_DIM)
        return jnp.einsum(
            "qhk,khd->qhd",
            weights.astype(jnp.bfloat16),
            value_heads,
            preferred_element_type=jnp.float32,
        )

    def absorb(state, key_block, value_block):
        row_peak, row_total, accumulated = state
        scores = scores_of(key_block)
        new_peak = jnp.maximum(row_peak, jnp.max(scores, axis=2))
        rescale = jnp.exp(row_peak - new_peak)
        weights = jnp.exp(scores - new_peak[..., None])
        row_total = row_total * rescale + jnp.sum(weights, axis=2)
        accumulated = accumulated * rescale[..., None] + weighted(weights, value_block)
        return (new_peak, row_total, accumulated)

    first_scores = scores_of(keys)
    first_peak = jnp.max(first_scores, axis=2)
    first_weights = jnp.exp(first_scores - first_peak[..., None])
    state = (first_peak, jnp.sum(first_weights, axis=2), weighted(first_weights, values))

    def step_ahead(key_block, value_block):
        return shifted((key_block, value_block), "blk", 1)

    def step_behind(key_block, value_block):
        return shifted((key_block, value_block), "blk", -1)

    block_count = lax.axis_size("blk")

    def one_turn(turn_index, carried):
        ahead_keys, ahead_values, behind_keys, behind_values, inner = carried
        ahead_keys, ahead_values = step_ahead(ahead_keys, ahead_values)
        behind_keys, behind_values = step_behind(behind_keys, behind_values)
        inner = absorb(inner, ahead_keys, ahead_values)
        inner = absorb(inner, behind_keys, behind_values)
        return (ahead_keys, ahead_values, behind_keys, behind_values, inner)

    carried = lax.fori_loop(0, block_count // 2 - 1, one_turn, (keys, values, keys, values, state))
    last_keys, last_values = step_ahead(carried[0], carried[1])
    row_peak, row_total, accumulated = absorb(carried[4], last_keys, last_values)
    peaks, totals, sums = (
        lax.all_to_all(row_peak[None], "team", split_axis=1, concat_axis=0, tiled=True),
        lax.all_to_all(row_total[None], "team", split_axis=1, concat_axis=0, tiled=True),
        lax.all_to_all(accumulated[None], "team", split_axis=1, concat_axis=0, tiled=True),
    )
    joint_peak = jnp.max(peaks, axis=0)
    rescale = jnp.exp(peaks - joint_peak[None])
    own_total = jnp.sum(totals * rescale, axis=0)
    own_sum = jnp.sum(sums * rescale[..., None], axis=0)
    attended = (own_sum / own_total[..., None]).astype(jnp.bfloat16)
    return attended.reshape(shard_rows, feature_width)


def solution(mesh):
    placed = (P(("team", "blk"), "head"), P(("team", "blk"), "head"), P(("team", "blk"), "head"))
    return jax.shard_map(
        on_device, mesh=mesh, in_specs=placed, out_specs=P(("team", "blk"), "head"), check_vma=False
    )
```

profile of v0, /device:TPU:0, one launch (start us, length us, event | category | flops | bytes accessed | tf_op | source)
XLA Modules:
  0.0 162.7 jit_solution(10376589958835616199)
XLA Ops:
  6.5 1.9 %copy.106 = bf16[128,1280]{0,1:T(8,128)(2,1)} copy(bf16[128,1280]{1,0:T(8,128)(2,1)} %param.3) | data formatting | bytes 655360 | tf_op args[0]
  8.4 1.2 copy.105
  9.6 3.0 %collective-permute-start = (bf16[128,1280]{0,1:T(8,128)(2,1)S(1)}, bf16[128,1280]{0,1:T(8,128)(2,1)S(1)}, u32[]{:S(2)}, u32[]{:S(2)}) collective-permute-start(bf16[128,1280]{0,1:T(8,128)(2,1)S(1)} %copy.105), channel_id=1, source_target_pairs={{0,2},{2,4},{4,6},{6,0},{1,3},{3,5},{5,7},{7,1},{8,10},{10,12},{12... | collective-permute-start | bytes 983048 | tf_op jit(solution)/shard_map/while/body/eval_jaxpr/ppermute | solution.py:12
  12.6 1.2 copy.109
  13.8 1.5 collective-permute-start.1
  15.4 1.4 collective-permute-start.2
  16.9 5.2 %collective-permute-done = bf16[128,1280]{0,1:T(8,128)(2,1)S(1)} collective-permute-done((bf16[128,1280]{0,1:T(8,128)(2,1)S(1)}, bf16[128,1280]{0,1:T(8,128)(2,1)S(1)}, u32[]{:S(2)}, u32[]{:S(2)}) %collective-permute-start) | collective-permute-done | bytes 327712 | tf_op jit(solution)/shard_map/while/body/eval_jaxpr/ppermute | solution.py:12
  22.1 1.1 collective-permute-start.4
  23.2 6.1 %collective-permute-done.1 = bf16[128,1280]{0,1:T(8,128)(2,1)} collective-permute-done((bf16[128,1280]{0,1:T(8,128)(2,1)S(1)}, bf16[128,1280]{0,1:T(8,128)(2,1)}, u32[]{:S(2)}, u32[]{:S(2)}) %collective-permute-start.1) | collective-permute-done | bytes 327712 | tf_op jit(solution)/shard_map/while/body/eval_jaxpr/ppermute | solution.py:12
  30.3 14.8 %all-gather.2.cloned.1.call-done = bf16[512,1280]{0,1:T(8,128)(2,1)} async-done(((bf16[128,1280]{0,1:T(8,128)(2,1)}), bf16[512,1280]{0,1:T(8,128)(2,1)}) %all-gather.2.cloned.1.call-update) | async-done | bytes 1310736 | tf_op jit(solution)/shard_map/all_gather | solution.py:20
  45.1 2.0 %bitcast_reduce_fusion.3 = (f32[512,10]{0,1:T(8,128)S(1)}, f32[10,128,512]{2,1,0:T(8,128)S(1)}) fusion(bf16[128,10,128]{0,2,1:T(8,128)(2,1)S(1)} %bitcast.149, bf16[512,10,128]{0,2,1:T(8,128)(2,1)} %bitcast.142), kind=kOutput, calls=%fused_computation.17 | convolution fusion | flops 169077760 | bytes 4280320 | tf_op jit(solution)/shard_map/qhd,khd->qhk/dot_general | solution.py:26
  48.3 1.9 %collective-permute-done.4 = bf16[128,1280]{0,1:T(8,128)(2,1)S(1)} collective-permute-done((bf16[128,1280]{0,1:T(8,128)(2,1)S(1)}, bf16[128,1280]{0,1:T(8,128)(2,1)S(1)}, u32[]{:S(2)}, u32[]{:S(2)}) %collective-permute-start.4) | collective-permute-done | bytes 327712 | tf_op jit(solution)/shard_map/ppermute | solution.py:12
  51.0 1.5 bitcast_reduce_fusion
  57.7 1.3 reduce.2
  59.8 5.3 %all-to-all-start.1 = ((f32[4,1,1280]{2,1,0:T(1,128)}), f32[4,1,1280]{2,1,0:T(1,128)S(1)}, u32[]{:S(2)}, u32[]{:S(2)}) async-start(f32[4,1,1280]{2,1,0:T(1,128)} %reshape.207), calls=%async_computation.1 | async-start | bytes 40960 | tf_op jit(solution)/shard_map/all_to_all | solution.py:74
  65.1 4.2 %fusion.16 = f32[10,512,128]{2,1,0:T(8,128)} fusion(bf16[128,10,128]{0,2,1:T(8,128)(2,1)} %bitcast.11, f32[10,128,512]{2,1,0:T(8,128)} %copy-done.4, f32[512,10]{0,1:T(8,128)} %copy-done.6), kind=kOutput, calls=%fused_computation.28 | convolution fusion | flops 169738240 | bytes 5591040 | tf_op jit(solution)/shard_map/while/body/eval_jaxpr/qhk,khd->qhd/dot_general | solution.py:32
  69.3 3.3 %fusion.18 = f32[10,512,128]{2,1,0:T(8,128)} fusion(bf16[128,10,128]{0,2,1:T(8,128)(2,1)} %bitcast.7, f32[10,128,512]{2,1,0:T(8,128)S(1)} %copy-done.3, f32[512,10]{0,1:T(8,128)S(1)} %get-tuple-element.24), kind=kOutput, calls=%fused_computation.29 | convolution fusion | flops 169738240 | bytes 5591040 | tf_op jit(solution)/shard_map/while/body/eval_jaxpr/qhk,khd->qhd/dot_general | solution.py:32
  72.7 2.2 %fusion.20 = f32[10,512,128]{2,1,0:T(8,128)} fusion(bf16[128,10,128]{0,2,1:T(8,128)(2,1)S(1)} %bitcast.151, f32[10,128,512]{2,1,0:T(8,128)S(1)} %copy-done.1, f32[512,10]{0,1:T(8,128)S(1)} %get-tuple-element.42), kind=kOutput, calls=%fused_computation.30 | convolution fusion | flops 169738240 | bytes 5591040 | tf_op jit(solution)/shard_map/qhk,khd->qhd/dot_general | solution.py:32
  75.0 1.3 reduce
  77.1 5.1 %all-to-all-start.2 = ((f32[4,1,1280]{2,1,0:T(1,128)}), f32[4,1,1280]{2,1,0:T(1,128)S(1)}, u32[]{:S(2)}, u32[]{:S(2)}) async-start(f32[4,1,1280]{2,1,0:T(1,128)} %reshape.209), calls=%async_computation.2 | async-start | bytes 40960 | tf_op jit(solution)/shard_map/all_to_all | solution.py:75
  82.2 5.5 %fusion = f32[1,512,10,128]{3,1,2,0:T(8,128)S(1)} fusion(f32[10,512,128]{2,1,0:T(8,128)} %fusion.16, f32[10,512,128]{2,1,0:T(8,128)} %fusion.18, f32[10,512,128]{2,1,0:T(8,128)} %fusion.20, bf16[128,10,128]{0,2,1:T(8,128)(2,1)} %bitcast.15, f32[10,128,512]{2,1,0:T(8,128)S(1)} %get-tuple-element.49, f32[512,10]{0,1:T(8,128)S(1)} %copy-done.9, ...), kind=kOutput, calls=%fused_computation.1 | convolution fusion | flops 173670400 | bytes 13516800 | tf_op jit(solution)/shard_map/qhk,khd->qhd/dot_general | solution.py:32
  87.7 4.2 %copy.128 = f32[1,512,10,128]{3,0,2,1:T(1,128)} copy(f32[1,512,10,128]{3,1,2,0:T(8,128)S(1)} %fusion) | data formatting | bytes 5242880 | tf_op jit(solution)/shard_map/broadcast_in_dim | solution.py:76
  92.0 5.1 %all-to-all-start = ((f32[1,512,10,128]{3,0,2,1:T(1,128)}), f32[1,512,10,128]{3,0,2,1:T(1,128)S(1)}, u32[]{:S(2)}, u32[]{:S(2)}) async-start(f32[1,512,10,128]{3,0,2,1:T(1,128)} %copy.128), calls=%async_computation | async-start | bytes 5242880 | tf_op jit(solution)/shard_map/all_to_all | solution.py:76
  99.6 53.8 %all-to-all-done = f32[1,512,10,128]{3,0,2,1:T(1,128)S(1)} async-done(((f32[1,512,10,128]{3,0,2,1:T(1,128)}), f32[1,512,10,128]{3,0,2,1:T(1,128)S(1)}, u32[]{:S(2)}, u32[]{:S(2)}) %all-to-all-start) | async-done | bytes 2621472 | tf_op jit(solution)/shard_map/all_to_all | solution.py:76
  (65 shorter events, 15.0 us)
Async XLA Ops:
  6.5 38.6 %all-gather.2.cloned.1.call-start = ((), (), s32[]{:S(2)}) async-start(), calls=%async_computation.3 | async-start | bytes 1638400 | tf_op jit(solution)/shard_map/all_gather | solution.py:20
  9.6 12.5 %collective-permute-start = (bf16[128,1280]{0,1:T(8,128)(2,1)S(1)}, bf16[128,1280]{0,1:T(8,128)(2,1)S(1)}, u32[]{:S(2)}, u32[]{:S(2)}) collective-permute-start(bf16[128,1280]{0,1:T(8,128)(2,1)S(1)} %copy.105), channel_id=1, source_target_pairs={{0,2},{2,4},{4,6},{6,0},{1,3},{3,5},{5,7},{7,1},{8,10},{10,12},{12... | collective-permute-start | bytes 983048 | tf_op jit(solution)/shard_map/while/body/eval_jaxpr/ppermute | solution.py:12
  13.8 15.5 %collective-permute-start.1 = (bf16[128,1280]{0,1:T(8,128)(2,1)S(1)}, bf16[128,1280]{0,1:T(8,128)(2,1)}, u32[]{:S(2)}, u32[]{:S(2)}) collective-permute-start(bf16[128,1280]{0,1:T(8,128)(2,1)S(1)} %copy.109), channel_id=1, source_target_pairs={{0,2},{2,4},{4,6},{6,0},{1,3},{3,5},{5,7},{7,1},{8,10},{10,12},{12... | collective-permute-start | bytes 983048 | tf_op jit(solution)/shard_map/while/body/eval_jaxpr/ppermute | solution.py:12
  15.4 32.4 %collective-permute-start.2 = (bf16[128,1280]{0,1:T(8,128)(2,1)S(1)}, bf16[128,1280]{0,1:T(8,128)(2,1)S(1)}, u32[]{:S(2)}, u32[]{:S(2)}) collective-permute-start(bf16[128,1280]{0,1:T(8,128)(2,1)S(1)} %copy.105), channel_id=1, source_target_pairs={{0,6},{2,0},{4,2},{6,4},{1,7},{3,1},{5,3},{7,5},{8,14},{10,8},{12,... | collective-permute-start | bytes 983048 | tf_op jit(solution)/shard_map/while/body/eval_jaxpr/ppermute | solution.py:12
  16.8 48.3 %collective-permute-start.3 = (bf16[128,1280]{0,1:T(8,128)(2,1)S(1)}, bf16[128,1280]{0,1:T(8,128)(2,1)}, u32[]{:S(2)}, u32[]{:S(2)}) collective-permute-start(bf16[128,1280]{0,1:T(8,128)(2,1)S(1)} %copy.109), channel_id=1, source_target_pairs={{0,6},{2,0},{4,2},{6,4},{1,7},{3,1},{5,3},{7,5},{8,14},{10,8},{12,... | collective-permute-start | bytes 983048 | tf_op jit(solution)/shard_map/while/body/eval_jaxpr/ppermute | solution.py:12
  22.1 28.1 %collective-permute-start.4 = (bf16[128,1280]{0,1:T(8,128)(2,1)S(1)}, bf16[128,1280]{0,1:T(8,128)(2,1)S(1)}, u32[]{:S(2)}, u32[]{:S(2)}) collective-permute-start(bf16[128,1280]{0,1:T(8,128)(2,1)S(1)} %collective-permute-done), channel_id=1, source_target_pairs={{0,2},{2,4},{4,6},{6,0},{1,3},{3,5},{5,7},{7,1},{8,10},{10,12},{12... | collective-permute-start | bytes 983048 | tf_op jit(solution)/shard_map/ppermute | solution.py:12
  29.3 52.9 %collective-permute-start.5 = (bf16[128,1280]{0,1:T(8,128)(2,1)}, bf16[128,1280]{0,1:T(8,128)(2,1)}, u32[]{:S(2)}, u32[]{:S(2)}) collective-permute-start(bf16[128,1280]{0,1:T(8,128)(2,1)} %collective-permute-done.1), channel_id=1, source_target_pairs={{0,2},{2,4},{4,6},{6,0},{1,3},{3,5},{5,7},{7,1},{8,10},{10,12},{12... | collective-permute-start | bytes 983048 | tf_op jit(solution)/shard_map/ppermute | solution.py:12
  45.1 2.0 %copy-start.5 = (bf16[512,1280]{0,1:T(8,128)(2,1)S(1)}, bf16[512,1280]{0,1:T(8,128)(2,1)}, u32[]{:S(2)}) copy-start(bf16[512,1280]{0,1:T(8,128)(2,1)} %all-gather.2.cloned.1.call-done) | copy-start | bytes 3932164
  47.1 7.8 %copy-start = (f32[10,128,512]{2,1,0:T(8,128)}, f32[10,128,512]{2,1,0:T(8,128)S(1)}, u32[]{:S(2)}) copy-start(f32[10,128,512]{2,1,0:T(8,128)S(1)} %get-tuple-element.43) | copy-start | bytes 7864324
  47.7 7.2 %copy-start.2 = (f32[10,128,512]{2,1,0:T(8,128)}, f32[10,128,512]{2,1,0:T(8,128)S(1)}, u32[]{:S(2)}) copy-start(f32[10,128,512]{2,1,0:T(8,128)S(1)} %get-tuple-element.45) | copy-start | bytes 7864324
  48.3 6.5 %copy-start.4 = (f32[10,128,512]{2,1,0:T(8,128)}, f32[10,128,512]{2,1,0:T(8,128)S(1)}, u32[]{:S(2)}) copy-start(f32[10,128,512]{2,1,0:T(8,128)S(1)} %get-tuple-element.47) | copy-start | bytes 7864324
  50.2 0.7 copy-start.7
  53.8 2.1 %copy-start.6 = (f32[512,10]{0,1:T(8,128)}, f32[512,10]{0,1:T(8,128)S(1)}, u32[]{:S(2)}) copy-start(f32[512,10]{0,1:T(8,128)S(1)} %get-tuple-element.26) | copy-start | bytes 61444
  54.4 1.5 copy-start.8
  59.8 17.3 %all-to-all-start.1 = ((f32[4,1,1280]{2,1,0:T(1,128)}), f32[4,1,1280]{2,1,0:T(1,128)S(1)}, u32[]{:S(2)}, u32[]{:S(2)}) async-start(f32[4,1,1280]{2,1,0:T(1,128)} %reshape.207), calls=%async_computation.1 | async-start | bytes 40960 | tf_op jit(solution)/shard_map/all_to_all | solution.py:74
  65.1 4.2 %copy-start.3 = (f32[10,128,512]{2,1,0:T(8,128)S(1)}, f32[10,128,512]{2,1,0:T(8,128)}, u32[]{:S(2)}) copy-start(f32[10,128,512]{2,1,0:T(8,128)} %copy-done.2) | copy-start | bytes 7864324
  69.3 3.3 %copy-start.1 = (f32[10,128,512]{2,1,0:T(8,128)S(1)}, f32[10,128,512]{2,1,0:T(8,128)}, u32[]{:S(2)}) copy-start(f32[10,128,512]{2,1,0:T(8,128)} %copy-done) | copy-start | bytes 7864324
  72.6 2.3 %copy-start.13 = (f32[1,512,10]{1,2,0:T(8,128)S(1)}, f32[1,512,10]{1,2,0:T(8,128)}, u32[]{:S(2)}) copy-start(f32[1,512,10]{1,2,0:T(8,128)} %get-tuple-element.41) | copy-start | bytes 61444
  72.6 9.6 %copy-start.9 = (f32[512,10]{0,1:T(8,128)S(1)}, f32[512,10]{0,1:T(8,128)}, u32[]{:S(2)}) copy-start(f32[512,10]{0,1:T(8,128)} %copy-done.8) | copy-start | bytes 61444
  72.6 9.6 %copy-start.10 = (f32[512,10]{0,1:T(8,128)S(1)}, f32[512,10]{0,1:T(8,128)}, u32[]{:S(2)}) copy-start(f32[512,10]{0,1:T(8,128)} %get-tuple-element.23) | copy-start | bytes 61444
  72.6 9.6 %copy-start.11 = (f32[512,10]{0,1:T(8,128)S(1)}, f32[512,10]{0,1:T(8,128)}, u32[]{:S(2)}) copy-start(f32[512,10]{0,1:T(8,128)} %get-tuple-element.25) | copy-start | bytes 61444
  72.6 9.6 %copy-start.12 = (f32[512,10]{0,1:T(8,128)S(1)}, f32[512,10]{0,1:T(8,128)}, u32[]{:S(2)}) copy-start(f32[512,10]{0,1:T(8,128)} %get-tuple-element.36) | copy-start | bytes 61444
  77.1 14.8 %all-to-all-start.2 = ((f32[4,1,1280]{2,1,0:T(1,128)}), f32[4,1,1280]{2,1,0:T(1,128)S(1)}, u32[]{:S(2)}, u32[]{:S(2)}) async-start(f32[4,1,1280]{2,1,0:T(1,128)} %reshape.209), calls=%async_computation.2 | async-start | bytes 40960 | tf_op jit(solution)/shard_map/all_to_all | solution.py:75
  92.0 61.4 %all-to-all-start = ((f32[1,512,10,128]{3,0,2,1:T(1,128)}), f32[1,512,10,128]{3,0,2,1:T(1,128)S(1)}, u32[]{:S(2)}, u32[]{:S(2)}) async-start(f32[1,512,10,128]{3,0,2,1:T(1,128)} %copy.128), calls=%async_computation | async-start | bytes 5242880 | tf_op jit(solution)/shard_map/all_to_all | solution.py:76
Sparse Core Ops, SparseCore 0:
  8.9 36.1 all-gather.1
where the time goes:
time: 163 us
  waiting for transfers between devices  81.8 us (50%)
  starting transfers between devices  23.8 us (15%)
  matrix products  19.9 us (12%)
  local copies, waits for them, and re-layouts  14 us (9%)
  between operations  13.7 us (8%)
  other arithmetic  9.52 us (6%)
    all_to_all x1, waiting for transfers between devices, on_device(): lax.all_to_all(accumulated[None], 'team', split_axis=1, concat_axis=0, ti...  53.8 us
    dot_general x4, matrix products, weighted(): jnp.einsum('qhk,khd->qhd', weights.astype(jnp.bfloat16), value_heads, pre...  15.2 us
    all_gather x1, waiting for transfers between devices, on_device(): team_query = lax.all_gather(query, 'team', axis=0, tiled=True)  14.8 us
    ppermute x6, waiting for transfers between devices, shifted(): lax.ppermute(value, axis, [(i, (i + by) % count) for i in range(count)])  13.2 us
    ppermute x6, starting transfers between devices, shifted(): lax.ppermute(value, axis, [(i, (i + by) % count) for i in range(count)])  8.25 us
    unnamed x37, local copies, waits for them, and re-layouts  8.02 us
    all_to_all x1, starting transfers between devices, on_device(): lax.all_to_all(row_peak[None], 'team', split_axis=1, concat_axis=0, tiled...  5.34 us
    all_to_all x1, starting transfers between devices, on_device(): lax.all_to_all(row_total[None], 'team', split_axis=1, concat_axis=0, tile...  5.09 us
  transfers between devices with their start and end apart: 10, of which 5 were waited for; matrix products, arithmetic and copies ran while one was open for 24% of the time, Pallas kernels for 0%

commit v1 on v0

--- a/solution.py
+++ b/solution.py
@@ -17,7 +17,12 @@
     feature_width = query.shape[1]
     head_count = feature_width // HEAD_DIM
     score_scale = 1.0 / math.sqrt(HEAD_DIM)
-    team_query = lax.all_gather(query, "team", axis=0, tiled=True)
+    ring = [query]
+    for hop in range(3):
+        ring.append(lax.ppermute(ring[-1], "team", [(dev, (dev + 1) % 4) for dev in range(4)]))
+    team_query = jnp.roll(
+        jnp.concatenate(ring[::-1], axis=0), (lax.axis_index("team") + 1) * ring[0].shape[0], axis=0
+    )
     team_heads = team_query.reshape(-1, head_count, HEAD_DIM)
 
     def scores_of(key_block):

time: 163 us -> 158 us (0.969)
  between operations: 13.7 us -> 0.36 us
  waiting for transfers between devices: 81.8 us -> 89.5 us
  starting transfers between devices: 23.8 us -> 26.3 us
    ppermute x0 -> x3, waiting for transfers between devices: none -> 15 us  [on_device(): lax.ppermute(ring[-1], 'team', [(dev, (dev + 1) % 4) for dev in range(4)])]
    all_gather x1 -> x0, waiting for transfers between devices: 14.8 us -> none  [on_device(): team_query = lax.all_gather(query, 'team', axis=0, tiled=True)]
    ppermute x6, waiting for transfers between devices: 13.2 us -> 22.4 us  [shifted(): lax.ppermute(value, axis, [(i, (i + by) % count) for i in range(count)])]
    ppermute x0 -> x3, starting transfers between devices: none -> 3.11 us  [on_device(): lax.ppermute(ring[-1], 'team', [(dev, (dev + 1) % 4) for dev in range(4)])]
    dot_general x4, matrix products: 4.68 us -> 2.29 us  [scores_of(): jnp.einsum('qhd,khd->qhk', team_heads, key_heads, preferred_element_type=...]
    all_to_all x1, waiting for transfers between devices: 53.8 us -> 52.1 us  [on_device(): lax.all_to_all(accumulated[None], 'team', split_axis=1, concat_axis=0, ti...]
    unnamed x37 -> x42, local copies, waits for them, and re-layouts: 8.02 us -> 7.34 us
  transfers between devices with their start and end apart: 10 -> 12, of which waited for: 5 -> 7; matrix products, arithmetic and copies ran while one was open for 24% -> 24% of each run, Pallas kernels for 0% -> 0%
where the time goes in v1:
time: 158 us
  waiting for transfers between devices  89.5 us (57%)
  starting transfers between devices  26.3 us (17%)
  matrix products  18.5 us (12%)
  local copies, waits for them, and re-layouts  13.6 us (9%)
  other arithmetic  9.52 us (6%)
    all_to_all x1, waiting for transfers between devices, on_device(): lax.all_to_all(accumulated[None], 'team', split_axis=1, concat_axis=0, ti...  52.1 us
    ppermute x6, waiting for transfers between devices, shifted(): lax.ppermute(value, axis, [(i, (i + by) % count) for i in range(count)])  22.4 us
    dot_general x4, matrix products, weighted(): jnp.einsum('qhk,khd->qhd', weights.astype(jnp.bfloat16), value_heads, pre...  16.2 us
    ppermute x3, waiting for transfers between devices, on_device(): lax.ppermute(ring[-1], 'team', [(dev, (dev + 1) % 4) for dev in range(4)])  15 us
    ppermute x6, starting transfers between devices, shifted(): lax.ppermute(value, axis, [(i, (i + by) % count) for i in range(count)])  7.93 us
    unnamed x42, local copies, waits for them, and re-layouts  7.34 us
    all_to_all x1, starting transfers between devices, on_device(): lax.all_to_all(row_total[None], 'team', split_axis=1, concat_axis=0, tile...  5.09 us
    all_to_all x1, starting transfers between devices, on_device(): lax.all_to_all(row_peak[None], 'team', split_axis=1, concat_axis=0, tiled...  5.09 us
  transfers between devices with their start and end apart: 12, of which 7 were waited for; matrix products, arithmetic and copies ran while one was open for 24% of the time, Pallas kernels for 0%

profile of v1, /device:TPU:0, one launch (start us, length us, event | category | flops | bytes accessed | tf_op | source)
XLA Modules:
  0.0 157.7 jit_solution(5831001619518844146)
XLA Ops:
  0.0 1.2 copy.111
  1.2 3.1 %collective-permute-start = (bf16[128,1280]{0,1:T(8,128)(2,1)S(1)}, bf16[128,1280]{0,1:T(8,128)(2,1)S(1)}, u32[]{:S(2)}, u32[]{:S(2)}) collective-permute-start(bf16[128,1280]{0,1:T(8,128)(2,1)S(1)} %copy.111), channel_id=1, source_target_pairs={{0,8},{8,16},{16,24},{24,0},{1,9},{9,17},{17,25},{25,1},{2,10},{10... | collective-permute-start | bytes 983048 | tf_op jit(solution)/shard_map/ppermute | solution.py:22
  4.3 9.7 %collective-permute-done = bf16[128,1280]{0,1:T(8,128)(2,1)S(1)} collective-permute-done((bf16[128,1280]{0,1:T(8,128)(2,1)S(1)}, bf16[128,1280]{0,1:T(8,128)(2,1)S(1)}, u32[]{:S(2)}, u32[]{:S(2)}) %collective-permute-start) | collective-permute-done | bytes 327712 | tf_op jit(solution)/shard_map/ppermute | solution.py:22
  14.0 1.2 copy.114
  15.2 1.5 collective-permute-start.3
  16.8 1.2 copy.117
  17.9 1.5 collective-permute-start.4
  19.5 5.2 %collective-permute-done.1 = bf16[128,1280]{0,1:T(8,128)(2,1)S(1)} collective-permute-done((bf16[128,1280]{0,1:T(8,128)(2,1)S(1)}, bf16[128,1280]{0,1:T(8,128)(2,1)S(1)}, u32[]{:S(2)}, u32[]{:S(2)}) %collective-permute-start.1) | collective-permute-done | bytes 327712 | tf_op jit(solution)/shard_map/ppermute | solution.py:22
  24.7 2.2 %collective-permute-start.5 = (bf16[128,1280]{0,1:T(8,128)(2,1)S(1)}, bf16[128,1280]{0,1:T(8,128)(2,1)S(1)}, u32[]{:S(2)}, u32[]{:S(2)}) collective-permute-start(bf16[128,1280]{0,1:T(8,128)(2,1)S(1)} %copy.114), channel_id=1, source_target_pairs={{0,6},{2,0},{4,2},{6,4},{1,7},{3,1},{5,3},{7,5},{8,14},{10,8},{12,... | collective-permute-start | bytes 983048 | tf_op jit(solution)/shard_map/while/body/eval_jaxpr/ppermute | solution.py:12
  27.5 1.5 collective-permute-start.7
  29.0 4.9 %collective-permute-done.4 = bf16[128,1280]{0,1:T(8,128)(2,1)} collective-permute-done((bf16[128,1280]{0,1:T(8,128)(2,1)S(1)}, bf16[128,1280]{0,1:T(8,128)(2,1)}, u32[]{:S(2)}, u32[]{:S(2)}) %collective-permute-start.4) | collective-permute-done | bytes 327712 | tf_op jit(solution)/shard_map/while/body/eval_jaxpr/ppermute | solution.py:12
  36.8 4.1 %collective-permute-done.5 = bf16[128,1280]{0,1:T(8,128)(2,1)S(1)} collective-permute-done((bf16[128,1280]{0,1:T(8,128)(2,1)S(1)}, bf16[128,1280]{0,1:T(8,128)(2,1)S(1)}, u32[]{:S(2)}, u32[]{:S(2)}) %collective-permute-start.5) | collective-permute-done | bytes 327712 | tf_op jit(solution)/shard_map/while/body/eval_jaxpr/ppermute | solution.py:12
  41.4 13.4 %collective-permute-done.7 = bf16[128,1280]{0,1:T(8,128)(2,1)S(1)} collective-permute-done((bf16[128,1280]{0,1:T(8,128)(2,1)S(1)}, bf16[128,1280]{0,1:T(8,128)(2,1)S(1)}, u32[]{:S(2)}, u32[]{:S(2)}) %collective-permute-start.7) | collective-permute-done | bytes 327712 | tf_op jit(solution)/shard_map/ppermute | solution.py:12
  60.6 1.3 reduce.2
  62.6 5.1 %all-to-all-start.1 = ((f32[4,1,1280]{2,1,0:T(1,128)}), f32[4,1,1280]{2,1,0:T(1,128)S(1)}, u32[]{:S(2)}, u32[]{:S(2)}) async-start(f32[4,1,1280]{2,1,0:T(1,128)} %reshape.207), calls=%async_computation.1 | async-start | bytes 40960 | tf_op jit(solution)/shard_map/all_to_all | solution.py:79
  67.7 4.1 %fusion.20 = f32[10,512,128]{2,1,0:T(8,128)} fusion(bf16[128,10,128]{0,2,1:T(8,128)(2,1)S(1)} %bitcast.151, f32[10,512,128]{1,2,0:T(8,128)} %copy-done.4, f32[512,10]{0,1:T(8,128)S(1)} %get-tuple-element.42), kind=kOutput, calls=%fused_computation.30 | convolution fusion | flops 169738240 | bytes 5591040 | tf_op jit(solution)/shard_map/qhk,khd->qhd/dot_general | solution.py:37
  71.8 3.3 %fusion.18 = f32[10,512,128]{2,1,0:T(8,128)} fusion(bf16[128,10,128]{0,2,1:T(8,128)(2,1)} %bitcast.7, f32[10,512,128]{1,2,0:T(8,128)S(1)} %copy-done.1, f32[512,10]{0,1:T(8,128)S(1)} %copy-done.6), kind=kOutput, calls=%fused_computation.29 | convolution fusion | flops 169738240 | bytes 5591040 | tf_op jit(solution)/shard_map/while/body/eval_jaxpr/qhk,khd->qhd/dot_general | solution.py:37
  75.2 3.2 %fusion.16 = f32[10,512,128]{2,1,0:T(8,128)} fusion(bf16[128,10,128]{0,2,1:T(8,128)(2,1)} %bitcast.11, f32[10,512,128]{1,2,0:T(8,128)S(1)} %copy-done.3, f32[512,10]{0,1:T(8,128)S(1)} %get-tuple-element.26), kind=kOutput, calls=%fused_computation.28 | convolution fusion | flops 169738240 | bytes 5591040 | tf_op jit(solution)/shard_map/while/body/eval_jaxpr/qhk,khd->qhd/dot_general | solution.py:37
  78.6 1.3 reduce
  80.7 5.1 %all-to-all-start.2 = ((f32[4,1,1280]{2,1,0:T(1,128)}), f32[4,1,1280]{2,1,0:T(1,128)S(1)}, u32[]{:S(2)}, u32[]{:S(2)}) async-start(f32[4,1,1280]{2,1,0:T(1,128)} %reshape.209), calls=%async_computation.2 | async-start | bytes 40960 | tf_op jit(solution)/shard_map/all_to_all | solution.py:80
  85.8 5.5 %fusion = f32[1,512,10,128]{3,1,2,0:T(8,128)S(1)} fusion(f32[10,512,128]{2,1,0:T(8,128)} %fusion.16, f32[10,512,128]{2,1,0:T(8,128)} %fusion.18, f32[10,512,128]{2,1,0:T(8,128)} %fusion.20, bf16[128,10,128]{0,2,1:T(8,128)(2,1)} %bitcast.15, f32[10,512,128]{1,2,0:T(8,128)S(1)} %get-tuple-element.49, f32[512,10]{0,1:T(8,128)S(1)} %copy-done.8, ...), kind=kOutput, calls=%fused_computation.1 | convolution fusion | flops 173670400 | bytes 13516800 | tf_op jit(solution)/shard_map/qhk,khd->qhd/dot_general | solution.py:37
  91.3 4.2 %copy.136 = f32[1,512,10,128]{3,0,2,1:T(1,128)} copy(f32[1,512,10,128]{3,1,2,0:T(8,128)S(1)} %fusion) | data formatting | bytes 5242880 | tf_op jit(solution)/shard_map/broadcast_in_dim | solution.py:81
  95.5 5.1 %all-to-all-start = ((f32[1,512,10,128]{3,0,2,1:T(1,128)}), f32[1,512,10,128]{3,0,2,1:T(1,128)S(1)}, u32[]{:S(2)}, u32[]{:S(2)}) async-start(f32[1,512,10,128]{3,0,2,1:T(1,128)} %copy.136), calls=%async_computation | async-start | bytes 5242880 | tf_op jit(solution)/shard_map/all_to_all | solution.py:81
  103.2 52.1 %all-to-all-done = f32[1,512,10,128]{3,0,2,1:T(1,128)S(1)} async-done(((f32[1,512,10,128]{3,0,2,1:T(1,128)}), f32[1,512,10,128]{3,0,2,1:T(1,128)S(1)}, u32[]{:S(2)}, u32[]{:S(2)}) %all-to-all-start) | async-done | bytes 2621472 | tf_op jit(solution)/shard_map/all_to_all | solution.py:81
  (75 shorter events, 16.3 us)
Async XLA Ops:
  1.2 12.8 %collective-permute-start = (bf16[128,1280]{0,1:T(8,128)(2,1)S(1)}, bf16[128,1280]{0,1:T(8,128)(2,1)S(1)}, u32[]{:S(2)}, u32[]{:S(2)}) collective-permute-start(bf16[128,1280]{0,1:T(8,128)(2,1)S(1)} %copy.111), channel_id=1, source_target_pairs={{0,8},{8,16},{16,24},{24,0},{1,9},{9,17},{17,25},{25,1},{2,10},{10... | collective-permute-start | bytes 983048 | tf_op jit(solution)/shard_map/ppermute | solution.py:22
  14.0 10.7 %collective-permute-start.1 = (bf16[128,1280]{0,1:T(8,128)(2,1)S(1)}, bf16[128,1280]{0,1:T(8,128)(2,1)S(1)}, u32[]{:S(2)}, u32[]{:S(2)}) collective-permute-start(bf16[128,1280]{0,1:T(8,128)(2,1)S(1)} %collective-permute-done), channel_id=1, source_target_pairs={{0,8},{8,16},{16,24},{24,0},{1,9},{9,17},{17,25},{25,1},{2,10},{10... | collective-permute-start | bytes 983048 | tf_op jit(solution)/shard_map/ppermute | solution.py:22
  15.2 12.3 %collective-permute-start.3 = (bf16[128,1280]{0,1:T(8,128)(2,1)S(1)}, bf16[128,1280]{0,1:T(8,128)(2,1)S(1)}, u32[]{:S(2)}, u32[]{:S(2)}) collective-permute-start(bf16[128,1280]{0,1:T(8,128)(2,1)S(1)} %copy.114), channel_id=1, source_target_pairs={{0,2},{2,4},{4,6},{6,0},{1,3},{3,5},{5,7},{7,1},{8,10},{10,12},{12... | collective-permute-start | bytes 983048 | tf_op jit(solution)/shard_map/while/body/eval_jaxpr/ppermute | solution.py:12
  17.9 15.9 %collective-permute-start.4 = (bf16[128,1280]{0,1:T(8,128)(2,1)S(1)}, bf16[128,1280]{0,1:T(8,128)(2,1)}, u32[]{:S(2)}, u32[]{:S(2)}) collective-permute-start(bf16[128,1280]{0,1:T(8,128)(2,1)S(1)} %copy.117), channel_id=1, source_target_pairs={{0,2},{2,4},{4,6},{6,0},{1,3},{3,5},{5,7},{7,1},{8,10},{10,12},{12... | collective-permute-start | bytes 983048 | tf_op jit(solution)/shard_map/while/body/eval_jaxpr/ppermute | solution.py:12
  24.7 9.8 %collective-permute-start.2 = (bf16[128,1280]{0,1:T(8,128)(2,1)S(1)}, bf16[128,1280]{0,1:T(8,128)(2,1)S(1)}, u32[]{:S(2)}, u32[]{:S(2)}) collective-permute-start(bf16[128,1280]{0,1:T(8,128)(2,1)S(1)} %collective-permute-done.1), channel_id=1, source_target_pairs={{0,8},{8,16},{16,24},{24,0},{1,9},{9,17},{17,25},{25,1},{2,10},{10... | collective-permute-start | bytes 983048 | tf_op jit(solution)/shard_map/ppermute | solution.py:22
  24.7 16.1 %collective-permute-start.5 = (bf16[128,1280]{0,1:T(8,128)(2,1)S(1)}, bf16[128,1280]{0,1:T(8,128)(2,1)S(1)}, u32[]{:S(2)}, u32[]{:S(2)}) collective-permute-start(bf16[128,1280]{0,1:T(8,128)(2,1)S(1)} %copy.114), channel_id=1, source_target_pairs={{0,6},{2,0},{4,2},{6,4},{1,7},{3,1},{5,3},{7,5},{8,14},{10,8},{12,... | collective-permute-start | bytes 983048 | tf_op jit(solution)/shard_map/while/body/eval_jaxpr/ppermute | solution.py:12
  26.9 48.2 %collective-permute-start.6 = (bf16[128,1280]{0,1:T(8,128)(2,1)S(1)}, bf16[128,1280]{0,1:T(8,128)(2,1)}, u32[]{:S(2)}, u32[]{:S(2)}) collective-permute-start(bf16[128,1280]{0,1:T(8,128)(2,1)S(1)} %copy.117), channel_id=1, source_target_pairs={{0,6},{2,0},{4,2},{6,4},{1,7},{3,1},{5,3},{7,5},{8,14},{10,8},{12,... | collective-permute-start | bytes 983048 | tf_op jit(solution)/shard_map/while/body/eval_jaxpr/ppermute | solution.py:12
  27.5 27.4 %collective-permute-start.7 = (bf16[128,1280]{0,1:T(8,128)(2,1)S(1)}, bf16[128,1280]{0,1:T(8,128)(2,1)S(1)}, u32[]{:S(2)}, u32[]{:S(2)}) collective-permute-start(bf16[128,1280]{0,1:T(8,128)(2,1)S(1)} %collective-permute-done.3), channel_id=1, source_target_pairs={{0,2},{2,4},{4,6},{6,0},{1,3},{3,5},{5,7},{7,1},{8,10},{10,12},{12... | collective-permute-start | bytes 983048 | tf_op jit(solution)/shard_map/ppermute | solution.py:12
  33.9 51.9 %collective-permute-start.8 = (bf16[128,1280]{0,1:T(8,128)(2,1)}, bf16[128,1280]{0,1:T(8,128)(2,1)}, u32[]{:S(2)}, u32[]{:S(2)}) collective-permute-start(bf16[128,1280]{0,1:T(8,128)(2,1)} %collective-permute-done.4), channel_id=1, source_target_pairs={{0,2},{2,4},{4,6},{6,0},{1,3},{3,5},{5,7},{7,1},{8,10},{10,12},{12... | collective-permute-start | bytes 983048 | tf_op jit(solution)/shard_map/ppermute | solution.py:12
  36.2 21.6 %copy-start = (f32[10,512,128]{1,2,0:T(8,128)}, f32[10,512,128]{1,2,0:T(8,128)S(1)}, u32[]{:S(2)}) copy-start(f32[10,512,128]{1,2,0:T(8,128)S(1)} %get-tuple-element.45) | copy-start | bytes 7864324
  36.8 21.0 %copy-start.4 = (f32[10,512,128]{1,2,0:T(8,128)}, f32[10,512,128]{1,2,0:T(8,128)S(1)}, u32[]{:S(2)}) copy-start(f32[10,512,128]{1,2,0:T(8,128)S(1)} %get-tuple-element.43) | copy-start | bytes 7864324
  41.4 15.7 %copy-start.2 = (f32[10,512,128]{1,2,0:T(8,128)}, f32[10,512,128]{1,2,0:T(8,128)S(1)}, u32[]{:S(2)}) copy-start(f32[10,512,128]{1,2,0:T(8,128)S(1)} %get-tuple-element.47) | copy-start | bytes 7864324
  56.0 2.7 %copy-start.5 = (f32[512,10]{0,1:T(8,128)}, f32[512,10]{0,1:T(8,128)S(1)}, u32[]{:S(2)}) copy-start(f32[512,10]{0,1:T(8,128)S(1)} %get-tuple-element.24) | copy-start | bytes 61444
  62.6 18.1 %all-to-all-start.1 = ((f32[4,1,1280]{2,1,0:T(1,128)}), f32[4,1,1280]{2,1,0:T(1,128)S(1)}, u32[]{:S(2)}, u32[]{:S(2)}) async-start(f32[4,1,1280]{2,1,0:T(1,128)} %reshape.207), calls=%async_computation.1 | async-start | bytes 40960 | tf_op jit(solution)/shard_map/all_to_all | solution.py:79
  67.7 4.1 %copy-start.1 = (f32[10,512,128]{1,2,0:T(8,128)S(1)}, f32[10,512,128]{1,2,0:T(8,128)}, u32[]{:S(2)}) copy-start(f32[10,512,128]{1,2,0:T(8,128)} %copy-done) | copy-start | bytes 7864324
  67.7 4.1 %copy-start.6 = (f32[512,10]{0,1:T(8,128)S(1)}, f32[512,10]{0,1:T(8,128)}, u32[]{:S(2)}) copy-start(f32[512,10]{0,1:T(8,128)} %copy-done.5) | copy-start | bytes 61444
  71.8 3.3 %copy-start.3 = (f32[10,512,128]{1,2,0:T(8,128)S(1)}, f32[10,512,128]{1,2,0:T(8,128)}, u32[]{:S(2)}) copy-start(f32[10,512,128]{1,2,0:T(8,128)} %copy-done.2) | copy-start | bytes 7864324
  75.2 3.3 %copy-start.12 = (f32[1,512,10]{1,2,0:T(8,128)S(1)}, f32[1,512,10]{1,2,0:T(8,128)}, u32[]{:S(2)}) copy-start(f32[1,512,10]{1,2,0:T(8,128)} %get-tuple-element.41) | copy-start | bytes 61444
  75.2 10.6 %copy-start.8 = (f32[512,10]{0,1:T(8,128)S(1)}, f32[512,10]{0,1:T(8,128)}, u32[]{:S(2)}) copy-start(f32[512,10]{0,1:T(8,128)} %copy-done.7) | copy-start | bytes 61444
  75.2 10.6 %copy-start.9 = (f32[512,10]{0,1:T(8,128)S(1)}, f32[512,10]{0,1:T(8,128)}, u32[]{:S(2)}) copy-start(f32[512,10]{0,1:T(8,128)} %get-tuple-element.23) | copy-start | bytes 61444
  75.2 10.6 %copy-start.10 = (f32[512,10]{0,1:T(8,128)S(1)}, f32[512,10]{0,1:T(8,128)}, u32[]{:S(2)}) copy-start(f32[512,10]{0,1:T(8,128)} %get-tuple-element.25) | copy-start | bytes 61444
  75.2 10.6 %copy-start.11 = (f32[512,10]{0,1:T(8,128)S(1)}, f32[512,10]{0,1:T(8,128)}, u32[]{:S(2)}) copy-start(f32[512,10]{0,1:T(8,128)} %get-tuple-element.36) | copy-start | bytes 61444
  80.7 14.8 %all-to-all-start.2 = ((f32[4,1,1280]{2,1,0:T(1,128)}), f32[4,1,1280]{2,1,0:T(1,128)S(1)}, u32[]{:S(2)}, u32[]{:S(2)}) async-start(f32[4,1,1280]{2,1,0:T(1,128)} %reshape.209), calls=%async_computation.2 | async-start | bytes 40960 | tf_op jit(solution)/shard_map/all_to_all | solution.py:80
  95.5 59.7 %all-to-all-start = ((f32[1,512,10,128]{3,0,2,1:T(1,128)}), f32[1,512,10,128]{3,0,2,1:T(1,128)S(1)}, u32[]{:S(2)}, u32[]{:S(2)}) async-start(f32[1,512,10,128]{3,0,2,1:T(1,128)} %copy.136), calls=%async_computation | async-start | bytes 5242880 | tf_op jit(solution)/shard_map/all_to_all | solution.py:81
  (1 other events, 1.0 us)
